TPU v7x, 128 devices: a whole 4x4x4 slice. The times are simulated.
128 devices in a mesh: seq: 8 (over x, z_hi), role: 2 (over z_lo), exp: 8 (over y, core).
Axes of the slice: x: 4, y: 4, z: 4 (z_hi: 2, z_lo: 2; z = z_hi * 2 + z_lo), core: 2. Of those that a mesh axis runs over, the one named last changes fastest.
Arguments:
- tokens: bfloat16 [2, 65536, 768], P(None, ('seq', 'role', 'exp')), may hold values from -6 to 6
- expert_ids: int32 [2, 65536, 1], P(None, ('seq', 'role', 'exp')), may hold values from 0 to 127; in each aligned block of 512 rows (0 to 511, 512 to 1023, ..., all dimensions but the last counted through in order) at most 8 rows name the same one
- attn_qkv: bfloat16 [768, 2304], P(('seq', 'role')), may hold values from -0.21875 to 0.21875
- attn_out: bfloat16 [768, 768], P(('seq', 'role')), may hold values from -0.21875 to 0.21875
- norm_attn: float32 [768], replicated, may hold values from 0.1 to 1.9
- norm_ffn: float32 [768], replicated, may hold values from 0.1 to 1.9
- router: bfloat16 [768, 128], replicated, may hold values from -0.43164062 to 0.43164062
- expert_in: bfloat16 [128, 768, 3072], P(('seq', 'role', 'exp')), may hold values from -0.21875 to 0.21875
- expert_out: bfloat16 [128, 3072, 768], P(('seq', 'role', 'exp')), may hold values from -0.109375 to 0.109375
Outputs:
- layer_out: bfloat16 [2, 65536, 768], P(None, ('seq', 'role', 'exp'))
Inputs may be any that keep to these rules, and one draw needn't show every extreme that they name: `expert_ids`: in each micro-batch the 512 tokens of one device name any one expert at most 8 times.
All inputs are finite; a program needn't handle non-finite values.
Results may differ from a plain program's by a relative error of at most 0.0058.
Values may be sent and summed in bfloat16 or wider, within the bound.
No kernel may reach another device: no remote copies, remote signals or barrier semaphores. Data moves between devices by JAX's collectives and lax.ppermute only.
A program may use at most 128 MiB of HBM per device.

v0:
```python
import jax
import jax.numpy as jnp
from jax import lax
from jax.sharding import PartitionSpec as P

HEADS = 12
LEN = 512


def scale_rows(values, gain_vec):
    floats = values.astype(jnp.float32)
    return floats * lax.rsqrt(jnp.mean(floats * floats, -1, keepdims=True) + 1e-06) * gain_vec


def add_columns(source, weight_piece):
    return jnp.dot(source, weight_piece, preferred_element_type=jnp.float32)


def body(
    tokens, expert_ids, attn_qkv, attn_out, norm_attn, norm_ffn, router, expert_in, expert_out
):
    batch_count, row_count, model_width = tokens.shape
    token_count = batch_count * row_count
    head_dim = model_width // HEADS
    flat_tokens = tokens.reshape(token_count, model_width)
    normed = scale_rows(flat_tokens, norm_attn).astype(jnp.bfloat16)
    projected = add_columns(
        normed, lax.all_gather(attn_qkv, ("seq", "role"), axis=0, tiled=True)
    ).astype(jnp.bfloat16)
    heads_split = projected.reshape(token_count // LEN, LEN, 3, HEADS, head_dim)

    def attend(sequence):
        scores = jnp.einsum(
            "qhd,khd->hqk", sequence[:, 0], sequence[:, 1], preferred_element_type=jnp.float32
        ) * head_dim ** (-0.5)
        weights = jnp.exp(scores)
        weights_norm = (weights / jnp.sum(weights, -1, keepdims=True)).astype(jnp.bfloat16)
        return jnp.einsum(
            "hqk,khd->qhd", weights_norm, sequence[:, 2], preferred_element_type=jnp.float32
        ).astype(jnp.bfloat16)

    context = lax.map(attend, heads_split).reshape(token_count, model_width)
    mixed = add_columns(context, lax.all_gather(attn_out, ("seq", "role"), axis=0, tiled=True))
    attended = (flat_tokens.astype(jnp.float32) + mixed).astype(jnp.bfloat16)
    normed_ffn = scale_rows(attended, norm_ffn).astype(jnp.bfloat16)
    experts = lax.axis_size(("seq", "role", "exp"))
    capacity = max(2, 2 * row_count // experts)
    chosen_ids = expert_ids.reshape(token_count)
    logits = jnp.dot(normed_ffn, router, preferred_element_type=jnp.float32)
    picked = chosen_ids[:, None] == lax.broadcasted_iota(jnp.int32, (1, experts), 1)
    gate_value = jax.nn.sigmoid(jnp.sum(jnp.where(picked, logits, 0.0), -1))
    marked = picked.reshape(batch_count, row_count, experts)
    triangle = (
        lax.broadcasted_iota(jnp.int32, (row_count, row_count), 0)
        >= lax.broadcasted_iota(jnp.int32, (row_count, row_count), 1)
    ).astype(jnp.bfloat16)
    running = jnp.einsum(
        "ij,bje->bie", triangle, marked.astype(jnp.bfloat16), preferred_element_type=jnp.float32
    )
    slot_index = jnp.sum(jnp.where(marked, running, 0.0), -1).astype(jnp.int32) - 1
    batch_index = lax.broadcasted_iota(jnp.int32, (batch_count, 1), 0)
    position = (
        chosen_ids.reshape(batch_count, row_count) * (batch_count * capacity)
        + batch_index * capacity
        + slot_index
    ).reshape(token_count)
    slots_total = experts * batch_count * capacity
    outgoing = jnp.zeros((slots_total, model_width), jnp.bfloat16).at[position].set(normed_ffn)
    outgoing = outgoing.reshape(experts, batch_count, capacity, model_width)
    weight_in = expert_in[0]
    weight_out = expert_out[0]
    rows_in = lax.all_to_all(
        outgoing, ("seq", "role", "exp"), split_axis=0, concat_axis=0, tiled=True
    )
    old_shape = rows_in.shape
    hidden = jax.nn.relu(
        jnp.dot(rows_in.reshape(-1, model_width), weight_in, preferred_element_type=jnp.float32)
    ).astype(jnp.bfloat16)
    returned_rows = lax.all_to_all(
        jnp.dot(hidden, weight_out, preferred_element_type=jnp.float32)
        .astype(jnp.bfloat16)
        .reshape(old_shape),
        ("seq", "role", "exp"),
        split_axis=0,
        concat_axis=0,
        tiled=True,
    )
    returned_rows = returned_rows.reshape(slots_total, model_width)
    result = returned_rows[position]
    layer_out = (
        attended.astype(jnp.float32) + gate_value[:, None] * result.astype(jnp.float32)
    ).astype(jnp.bfloat16)
    return layer_out.reshape(batch_count, row_count, model_width)


def solution(mesh):
    in_specs = (
        P(None, ("seq", "role", "exp"), None),
        P(None, ("seq", "role", "exp"), None),
        P(("seq", "role"), None),
        P(("seq", "role"), None),
        P(),
        P(),
        P(),
        P(("seq", "role", "exp"), None, None),
        P(("seq", "role", "exp"), None, None),
    )
    out_specs = P(None, ("seq", "role", "exp"), None)
    return jax.shard_map(body, mesh=mesh, in_specs=in_specs, out_specs=out_specs, check_vma=False)
```

profile of v0, /device:TPU:1, one launch (start us, length us, event | category | flops | bytes accessed | tf_op | source)
XLA Modules:
  0.0 254.4 jit_solution(380767495640874659)
XLA Ops:
  6.5 0.7 all-gather.3.cloned.1.call-update
  7.3 0.0 all-gather.5.cloned.1.call-start
  7.3 0.7 all-gather.5.cloned.1.call-update
  8.0 0.7 copy.23
  8.7 0.7 broadcast_multiply_fusion
  9.4 1.8 fusion.20
  11.2 0.4 fusion.28
  11.6 0.1 broadcast_bitcast_fusion
  11.7 1.6 fusion.22
  13.3 48.2 %all-gather.3.cloned.1.call-done = bf16[768,2304]{1,0:T(8,128)(2,1)} async-done(((bf16[48,2304]{1,0:T(8,128)(2,1)}), bf16[768,2304]{1,0:T(8,128)(2,1)}) %all-gather.3.cloned.1.call-update) | async-done | bytes 3538960 | tf_op jit(solution)/shard_map/all_gather | solution.py:28
  61.5 8.4 %convolution_convert_fusion = bf16[1024,2304]{1,0:T(8,128)(2,1)} fusion(bf16[1024,768]{1,0:T(8,128)(2,1)} %fusion.22, bf16[768,2304]{1,0:T(8,128)(2,1)} %all-gather.3.cloned.1.call-done), kind=kOutput, calls=%fused_computation.16 | convolution fusion | flops 3626237952 | bytes 9830400 | tf_op jit(solution)/shard_map/dot_general | solution.py:16
  69.9 6.7 %copy.13 = bf16[1024,2304]{0,1:T(8,128)(2,1)} copy(bf16[1024,2304]{1,0:T(8,128)(2,1)} %convolution_convert_fusion) | data formatting | bytes 9437184 | tf_op jit(solution)/shard_map/convert_element_type | solution.py:29
  76.6 8.8 %reshape.127 = bf16[2,512,3,12,64]{1,0,4,3,2:T(2,128)(2,1)} reshape(bf16[1024,2304]{0,1:T(8,128)(2,1)} %copy.13) | data formatting | bytes 9437184 | tf_op jit(solution)/shard_map/reshape | solution.py:30
  85.5 5.5 %copy.14 = bf16[2,512,3,12,64]{1,4,3,2,0:T(8,128)(2,1)} copy(bf16[2,512,3,12,64]{1,0,4,3,2:T(2,128)(2,1)} %reshape.127) | data formatting | bytes 9437184 | tf_op jit(solution)/shard_map/while | solution.py:42
  91.0 13.4 %while.10 = (s32[]{:T(128)}, bf16[2,512,12,64]{1,3,2,0:T(8,128)(2,1)S(1)}, bf16[2,512,3,12,64]{1,4,3,2,0:T(8,128)(2,1)}, s32[]{:T(128)}) while((s32[]{:T(128)}, bf16[2,512,12,64]{1,3,2,0:T(8,128)(2,1)S(1)}, bf16[2,512,3,12,64]{1,4,3,2,0:T(8,128)(2,1)}, s32[]{:T(128)}) %tuple.24), condition=%wide.region_3.4_spmd, body=%wide.region_1.3_spmd.sunk | while | flops 821422080 | bytes 33087548 | solution.py:42
  91.0 1.9 dynamic-slice_bitcast_fusion.2
  92.9 2.3 fusion.43
  95.2 2.4 fusion.44
  97.7 1.9 dynamic-slice_bitcast_fusion.2
  99.6 2.3 fusion.43
  102.0 2.4 fusion.44
  104.4 1.6 copy.15
  106.0 0.4 copy.19
  106.5 4.0 %fusion.16 = (f32[1024]{0:T(1024)S(1)}, bf16[1024,768]{1,0:T(8,128)(2,1)}) fusion(bf16[1024,768]{0,1:T(8,128)(2,1)S(1)} %bitcast.102, bf16[768,768]{1,0:T(8,128)(2,1)} %all-gather.5.cloned.1.call-done, bf16[2,512,768]{2,1,0:T(8,128)(2,1)S(1)} %copy-done.1), kind=kOutput, calls=%fused_computation.24 | convolution fusion | flops 1212677120 | bytes 5902336 | tf_op jit(solution)/shard_map/dot_general | solution.py:16
  110.5 7.2 %scatter_custom_fusion = bf16[2048,768]{1,0:T(8,128)(2,1)S(1)} fusion(s32[1024]{0:T(1024)S(1)} %bitcast.105, bf16[]{:T(256)} %constant.7.clone.1, bf16[1024,768]{1,0:T(8,128)(2,1)} %get-tuple-element.38, f32[768]{0:T(1024)S(1)} %copy-done.4, f32[1024]{0:T(1024)S(1)} %add_rsqrt_fusion), kind=kCustom, calls=%fused_computation.35 | custom fusion | flops 3145728 | bytes 4726786 | tf_op jit(solution)/shard_map/scatter | solution.py:68
  117.7 49.2 %all_to_all.10 = bf16[128,2,8,768]{3,2,1,0:T(8,128)(2,1)} all-to-all(bf16[128,2,8,768]{3,2,1,0:T(8,128)(2,1)S(1)} %bitcast.98), channel_id=1, replica_groups=mesh['seq'=8,'role'=2,'exp'=8] {'seq','role','exp'}, dimensions={0} | all-to-all | bytes 6291456 | tf_op jit(solution)/shard_map/all_to_all | solution.py:72
  166.9 25.4 %fusion.11 = bf16[2048,768]{1,0:T(8,128)(2,1)} fusion(bf16[1,3072,768]{2,1,0:T(8,128)(2,1)} %param.19, bf16[2048,768]{1,0:T(8,128)(2,1)} %bitcast.101, bf16[1,768,3072]{2,1,0:T(8,128)(2,1)} %param.18), kind=kOutput, calls=%fused_computation.23 | convolution fusion | flops 19341508608 | bytes 15728640 | tf_op jit(solution)/shard_map/dot_general | solution.py:80
  192.3 4.8 %all-to-all-start.1 = ((bf16[128,2,8,768]{3,2,1,0:T(8,128)(2,1)}), bf16[128,2,8,768]{3,2,1,0:T(8,128)(2,1)S(1)}, u32[]{:S(2)}, u32[]{:S(2)}) async-start(bf16[128,2,8,768]{3,2,1,0:T(8,128)(2,1)} %bitcast.100), calls=%async_computation.1 | async-start | bytes 6291456 | tf_op jit(solution)/shard_map/all_to_all | solution.py:79
  197.1 2.2 fusion.27
  199.3 39.5 %all-to-all-done.1 = bf16[128,2,8,768]{3,2,1,0:T(8,128)(2,1)S(1)} async-done(((bf16[128,2,8,768]{3,2,1,0:T(8,128)(2,1)}), bf16[128,2,8,768]{3,2,1,0:T(8,128)(2,1)S(1)}, u32[]{:S(2)}, u32[]{:S(2)}) %all-to-all-start.1) | async-done | bytes 3145760 | tf_op jit(solution)/shard_map/all_to_all | solution.py:79
  238.8 5.2 %gather_fusion = bf16[1024,768]{1,0:T(8,128)(2,1)} fusion(bf16[2048,768]{1,0:T(8,128)(2,1)S(1)} %bitcast.97, s32[1024]{0:T(1024)S(1)} %broadcast_clamp_fusion), kind=kCustom, calls=%fused_computation | custom fusion | bytes 3149824 | tf_op jit(solution)/shard_map/gather | solution.py:89
  244.0 3.5 %fusion.19 = bf16[1024,768]{1,0:T(8,128)(2,1)} fusion(bf16[1024,768]{1,0:T(8,128)(2,1)} %get-tuple-element.38, bf16[1024,768]{1,0:T(8,128)(2,1)} %gather_fusion, f32[1024]{0:T(1024)S(1)} %add_divide_fusion), kind=kLoop, calls=%fused_computation.27 | loop fusion | flops 3932160 | bytes 4722688 | tf_op jit(solution)/shard_map/convert_element_type | solution.py:92
  (23 shorter events, 0.1 us)
Async XLA Ops:
  6.5 190.6 %copy-start = (bf16[768,128]{1,0:T(8,128)(2,1)S(1)}, bf16[768,128]{1,0:T(8,128)(2,1)}, u32[]{:S(2)}) copy-start(bf16[768,128]{1,0:T(8,128)(2,1)} %param.17) | copy-start | bytes 589828
  6.5 5.2 %copy-start.1 = (bf16[2,512,768]{2,1,0:T(8,128)(2,1)S(1)}, bf16[2,512,768]{2,1,0:T(8,128)(2,1)}, u32[]{:S(2)}) copy-start(bf16[2,512,768]{2,1,0:T(8,128)(2,1)} %param.11) | copy-start | bytes 4718596
  6.5 5.2 %copy-start.3 = (f32[768]{0:T(1024)S(1)}, f32[768]{0:T(1024)}, u32[]{:S(2)}) copy-start(f32[768]{0:T(1024)} %param.15) | copy-start | bytes 9220
  6.5 55.0 %all-gather.3.cloned.1.call-start = ((), (), s32[]{:S(2)}) async-start(), calls=%async_computation.2 | async-start | bytes 3760128 | tf_op jit(solution)/shard_map/all_gather | solution.py:28
  7.3 99.2 %all-gather.5.cloned.1.call-start = ((), (), s32[]{:S(2)}) async-start(), calls=%async_computation.3 | async-start | bytes 1253376 | tf_op jit(solution)/shard_map/all_gather | solution.py:43
  106.5 4.0 %copy-start.4 = (f32[768]{0:T(1024)S(1)}, f32[768]{0:T(1024)}, u32[]{:S(2)}) copy-start(f32[768]{0:T(1024)} %param.16) | copy-start | bytes 9220
  192.3 4.8 %copy-start.2 = (s32[2,512,1]{1,2,0:T(1,128)S(1)}, s32[2,512,1]{1,2,0:T(1,128)}, u32[]{:S(2)}) copy-start(s32[2,512,1]{1,2,0:T(1,128)} %param.12) | copy-start | bytes 12292
  192.3 46.5 %all-to-all-start.1 = ((bf16[128,2,8,768]{3,2,1,0:T(8,128)(2,1)}), bf16[128,2,8,768]{3,2,1,0:T(8,128)(2,1)S(1)}, u32[]{:S(2)}, u32[]{:S(2)}) async-start(bf16[128,2,8,768]{3,2,1,0:T(8,128)(2,1)} %bitcast.100), calls=%async_computation.1 | async-start | bytes 6291456 | tf_op jit(solution)/shard_map/all_to_all | solution.py:79
Sparse Core Ops, SparseCore 0:
  9.5 51.9 all-gather.2
  63.7 40.5 all-gather.4
where the time goes:
time: 255 us; the launch traced here: 254 us
  waiting for transfers between devices  89.1 us (35%)
  matrix products  49.9 us (20%)
  blocking collectives  49.2 us (19%)
  local copies, waits for them, and re-layouts  33 us (13%)
  other arithmetic  14.9 us (6%)
  between operations  13.6 us (5%)
  starting transfers between devices  4.79 us (2%)
    all_to_all x1, blocking collectives, body(): lax.all_to_all(outgoing, ('seq', 'role', 'exp'), split_axis=0, concat_axi...  49.2 us
    all_gather x1, waiting for transfers between devices, body(): lax.all_gather(attn_qkv, ('seq', 'role'), axis=0, tiled=True)  48.2 us
    all_to_all x1, waiting for transfers between devices, body(): lax.all_to_all(jnp.dot(hidden, weight_out, preferred_element_type=jnp.flo...  39.5 us
    dot_general x1, matrix products, body(): jnp.dot(hidden, weight_out, preferred_element_type=jnp.float32)  25.4 us
    dot_general x2, matrix products, add_columns(): return jnp.dot(source, weight_piece, preferred_element_type=jnp.float32)  12.4 us
    reshape x1, local copies, waits for them, and re-layouts, body(): heads_split = projected.reshape(token_count // LEN, LEN, 3, HEADS, head_dim)  8.81 us
    scatter x1, other arithmetic, body(): jnp.zeros((slots_total, model_width), jnp.bfloat16).at[position]  7.21 us
    while x2, local copies, waits for them, and re-layouts, body(): context = lax.map(attend, heads_split).reshape(token_count, model_width)  7.17 us
  transfers between devices with their start and end apart: 3, of which 2 were waited for; matrix products, arithmetic and copies ran while one was open for 21% of the time, Pallas kernels for 0%

commit v1 on v0

v1 whole, which is shorter than its diff:
```python
import functools

import jax
import jax.numpy as jnp
from jax import lax
from jax.experimental import pallas as pl
from jax.experimental.pallas import tpu as pltpu
from jax.sharding import PartitionSpec as P

HEADS = 12
HALF = 384
SLOTS = 8
ALL = ("seq", "role", "exp")
F32 = jnp.float32
BF16 = jnp.bfloat16


def place(x, z, y, c):
    return x * 32 + z * 8 + y * 2 + c


def hop(d, phase):
    pairs = []
    for x in range(4):
        for z in range(4):
            for y in range(4):
                for c in range(2):
                    if (c == 0) == (phase == 0):
                        to = place((x + d) % 4, z, y, c)
                    else:
                        to = place(x, (z + d) % 4, y, c)
                    pairs.append((place(x, z, y, c), to))
    return pairs


def my_core():
    return lax.rem(lax.axis_index("exp"), 2)


def scale_rows(values, gain):
    floats = values.astype(F32)
    return floats * lax.rsqrt(jnp.mean(floats * floats, -1, keepdims=True) + 1e-06) * gain


def assemble_kernel(b0, b1, b2, b3, w_ref, sem):
    seq = lax.axis_index("seq")
    x = seq // 2
    z = lax.rem(seq, 2) * 2 + lax.axis_index("role")
    core = my_core()
    shift = (0, 3, 1, 2)
    copies = []
    for i, block in enumerate((b0, b1, b2, b3)):
        for j in range(4):
            dx = jnp.where(core == 0, shift[j], shift[i])
            dz = jnp.where(core == 0, shift[i], shift[j])
            row = (lax.rem(x + dx, 4) * 4 + lax.rem(z + dz, 4)) * 48
            copies.append(
                pltpu.make_async_copy(
                    block.at[pl.ds(j * 48, 48), :],
                    w_ref.at[pl.ds(pl.multiple_of(row, 16), 48), :],
                    sem.at[i * 4 + j],
                )
            )
    for copy in copies:
        copy.start()
    for copy in copies:
        copy.wait()


def assemble(blocks):
    any_spec = pl.BlockSpec(memory_space=pl.ANY)
    return pl.pallas_call(
        assemble_kernel,
        out_shape=jax.ShapeDtypeStruct((768, blocks[0].shape[1]), BF16),
        in_specs=[any_spec] * 4,
        out_specs=any_spec,
        scratch_shapes=[pltpu.SemaphoreType.DMA((16,))],
        name="assemble",
    )(*blocks)


def half_context(normed, weights):
    rows = normed.shape[0]
    projected = jnp.dot(normed, weights, preferred_element_type=F32).astype(BF16)
    low = lax.broadcasted_iota(jnp.int32, (rows, 128), 1) < 64
    ones = jnp.ones((rows, 128), BF16)
    zero = jnp.zeros((rows, 128), BF16)
    pieces = []
    for pair in range(3):
        q = projected[:, pair * 128 : pair * 128 + 128] * jnp.asarray(0.125, BF16)
        k = projected[:, HALF + pair * 128 : HALF + pair * 128 + 128]
        v = projected[:, 2 * HALF + pair * 128 : 2 * HALF + pair * 128 + 128]
        values = jnp.concatenate([v, ones], axis=1)
        outs = []
        for side in range(2):
            mine = jnp.where(low, q, zero) if side == 0 else jnp.where(low, zero, q)
            scores = lax.dot_general(
                mine, k, (((1,), (1,)), ((), ())), preferred_element_type=F32
            )
            top = jnp.max(scores, -1, keepdims=True)
            weight = jnp.exp(scores - top).astype(BF16)
            total = jnp.dot(weight, values, preferred_element_type=F32)
            outs.append(total[:, :128] / total[:, 128:])
        pieces.append(jnp.where(low, outs[0], outs[1]).astype(BF16))
    return jnp.concatenate(pieces, axis=1)


def context_kernel(x_ref, gain_ref, w_ref, ctx_ref):
    normed = scale_rows(x_ref[0], gain_ref[...]).astype(BF16)
    ctx_ref[...] = half_context(normed, w_ref[:, : 3 * HALF])


def finish(x, ctx, w, gain, router, ids_row, ids_col, att_ref, out_ref, aux_ref):
    rows = x.shape[0]
    mixed = []
    for side in range(2):
        columns = w[side, :, 3 * HALF :]
        mixed.append(
            jnp.dot(ctx[0], columns[:HALF], preferred_element_type=F32)
            + jnp.dot(ctx[1], columns[HALF:], preferred_element_type=F32)
        )
    attended = (x.astype(F32) + jnp.concatenate(mixed, axis=1)).astype(BF16)
    att_ref[...] = attended
    normed = scale_rows(attended, gain).astype(BF16)
    experts = router.shape[1]
    logits = jnp.dot(normed, router, preferred_element_type=F32)
    i0 = lax.broadcasted_iota(jnp.int32, (rows, rows), 0)
    i1 = lax.broadcasted_iota(jnp.int32, (rows, rows), 1)
    picked = ids_col == lax.broadcasted_iota(jnp.int32, (rows, experts), 1)
    gate = jax.nn.sigmoid(jnp.sum(jnp.where(picked, logits, 0.0), -1, keepdims=True))
    running = jnp.dot(
        (i0 >= i1).astype(F32).astype(BF16),
        picked.astype(F32).astype(BF16),
        preferred_element_type=F32,
    )
    rank = jnp.sum(jnp.where(picked, running, 0.0), -1, keepdims=True)
    position = ids_col.astype(F32) * SLOTS + rank - 1.0
    aux_lane = lax.broadcasted_iota(jnp.int32, (rows, 128), 1)
    aux_ref[...] = jnp.where(aux_lane == 0, gate, position)
    picked_t = ids_row == lax.broadcasted_iota(jnp.int32, (experts, rows), 0)
    running_t = jnp.dot(
        picked_t.astype(F32).astype(BF16),
        (i0 <= i1).astype(F32).astype(BF16),
        preferred_element_type=F32,
    )
    rank_t = jnp.sum(jnp.where(picked_t, running_t, 0.0), 0, keepdims=True)
    position_t = ids_row * SLOTS + rank_t.astype(jnp.int32) - 1
    slots = experts * SLOTS
    spread = (lax.broadcasted_iota(jnp.int32, (slots, rows), 0) == position_t).astype(F32).astype(BF16)
    out_ref[...] = jnp.dot(spread, normed, preferred_element_type=F32).astype(BF16)


def load_weights(mine_ref, other_ref, w, sems):
    core = my_core()
    first = pltpu.make_async_copy(mine_ref, w.at[core], sems.at[0])
    second = pltpu.make_async_copy(other_ref, w.at[1 - core], sems.at[1])
    first.start()
    second.start()
    first.wait()
    second.wait()
    return core


def second_half_kernel(
    x_ref, gain_ref, mine_ref, other_ref, ctx_ref, gain2_ref, router_ref, row_ref, col_ref,
    att_ref, out_ref, aux_ref, w, ctx, sems,
):
    core = load_weights(mine_ref, other_ref, w, sems)
    normed = scale_rows(x_ref[0], gain_ref[...]).astype(BF16)
    ctx[core] = ctx_ref[...]
    ctx[1 - core] = half_context(normed, w[1 - core, :, : 3 * HALF])
    finish(
        x_ref[0], ctx, w, gain2_ref[...], router_ref[...], row_ref[0], col_ref[0],
        att_ref, out_ref, aux_ref,
    )


def whole_kernel(
    x_ref, gain_ref, mine_ref, other_ref, gain2_ref, router_ref, row_ref, col_ref,
    att_ref, out_ref, aux_ref, w, ctx, sems,
):
    load_weights(mine_ref, other_ref, w, sems)
    normed = scale_rows(x_ref[0], gain_ref[...]).astype(BF16)

    def step(side, carry):
        ctx[side] = half_context(normed, w[side, :, : 3 * HALF])
        return carry

    lax.fori_loop(0, 2, step, 0)
    finish(
        x_ref[0], ctx, w, gain2_ref[...], router_ref[...], row_ref[0], col_ref[0],
        att_ref, out_ref, aux_ref,
    )


def combine_kernel(att_ref, aux_ref, back_ref, out_ref):
    rows, slots = att_ref.shape[0], back_ref.shape[0]
    gate = aux_ref[:, 0:1]
    position = aux_ref[:, 1:2].astype(jnp.int32)
    pick = (lax.broadcasted_iota(jnp.int32, (rows, slots), 1) == position).astype(F32).astype(BF16)
    result = jnp.dot(pick, back_ref[...], preferred_element_type=F32)
    out_ref[0] = (att_ref[...].astype(F32) + gate * result).astype(BF16)


def combine_after_kernel(att_ref, aux_ref, back_ref, held_ref, out_ref):
    del held_ref
    combine_kernel(att_ref, aux_ref, back_ref, out_ref)


def full(shape):
    return pl.BlockSpec(shape, lambda i: (0,) * len(shape))


def body(
    tokens, expert_ids, attn_qkv, attn_out, norm_attn, norm_ffn, router, expert_in, expert_out
):
    batches, rows, width = tokens.shape
    experts = router.shape[1]
    slots = experts * SLOTS
    core = my_core()
    parts = attn_qkv.reshape(48, 3, 2, HALF)
    out_parts = attn_out.reshape(48, 1, 2, HALF)
    parts = jnp.concatenate([parts, out_parts], axis=1)
    piece = jnp.where(core == 0, parts[:, :, 0], parts[:, :, 1]).reshape(48, 4 * HALF)
    block = jnp.concatenate(
        [piece] + [lax.ppermute(piece, ALL, hop(d, 0)) for d in (1, -1, 2)], axis=0
    )
    others = [lax.ppermute(block, ALL, hop(d, 1)) for d in (1, -1, 2)]
    w_mine = assemble([block] + others)
    w_other = lax.ppermute(w_mine, ALL, [(i, i ^ 1) for i in range(128)])

    gain = norm_attn.reshape(1, width)
    gain2 = norm_ffn.reshape(1, width)
    ids_row = expert_ids.reshape(batches, 1, rows)

    def token_spec(b):
        return pl.BlockSpec((1, rows, width), lambda i: (b, 0, 0))

    any_spec = pl.BlockSpec(memory_space=pl.ANY)
    ctx_mine = pl.pallas_call(
        context_kernel,
        grid=(1,),
        out_shape=jax.ShapeDtypeStruct((rows, HALF), BF16),
        in_specs=[token_spec(0), full((1, width)), full((width, 4 * HALF))],
        out_specs=full((rows, HALF)),
        name="first_half",
    )(tokens, gain, w_mine)

    finish_out = (
        jax.ShapeDtypeStruct((rows, width), BF16),
        jax.ShapeDtypeStruct((slots, width), BF16),
        jax.ShapeDtypeStruct((rows, 128), F32),
    )
    finish_specs = (full((rows, width)), full((slots, width)), full((rows, 128)))
    scratch = [
        pltpu.VMEM((2, width, 4 * HALF), BF16),
        pltpu.VMEM((2, rows, HALF), BF16),
        pltpu.SemaphoreType.DMA((2,)),
    ]

    def tail_specs(b):
        return [
            full((1, width)),
            full((width, experts)),
            pl.BlockSpec((1, 1, rows), lambda i: (b, 0, 0)),
            pl.BlockSpec((1, rows, 1), lambda i: (b, 0, 0)),
        ]

    first = pl.pallas_call(
        second_half_kernel,
        grid=(1,),
        out_shape=finish_out,
        in_specs=[token_spec(0), full((1, width)), any_spec, any_spec, full((rows, HALF))]
        + tail_specs(0),
        out_specs=finish_specs,
        scratch_shapes=scratch,
        name="second_half",
    )(tokens, gain, w_mine, w_other, ctx_mine, gain2, router, ids_row, expert_ids)

    second = pl.pallas_call(
        whole_kernel,
        grid=(1,),
        out_shape=finish_out,
        in_specs=[token_spec(1), full((1, width)), any_spec, any_spec] + tail_specs(1),
        out_specs=finish_specs,
        scratch_shapes=scratch,
        name="whole",
    )(tokens, gain, w_mine, w_other, gain2, router, ids_row, expert_ids)

    weight_in = expert_in[0]
    weight_out = expert_out[0]

    def exchange(values):
        return lax.all_to_all(
            values.reshape(experts, SLOTS, width), ALL, split_axis=0, concat_axis=0, tiled=True
        ).reshape(slots, width)

    def serve(values):
        hidden = jax.nn.relu(jnp.dot(values, weight_in, preferred_element_type=F32)).astype(BF16)
        return jnp.dot(hidden, weight_out, preferred_element_type=F32).astype(BF16)

    arrived = [exchange(first[1]), exchange(second[1])]
    back = [exchange(serve(values)) for values in arrived]

    out_shape = jax.ShapeDtypeStruct((batches, rows, width), BF16)
    specs = [full((rows, width)), full((rows, 128)), full((slots, width))]
    held = pl.pallas_call(
        combine_kernel,
        grid=(1,),
        out_shape=out_shape,
        in_specs=specs,
        out_specs=token_spec(0),
        name="combine0",
    )(first[0], first[2], back[0])
    return pl.pallas_call(
        combine_after_kernel,
        grid=(1,),
        out_shape=out_shape,
        in_specs=specs + [any_spec],
        out_specs=token_spec(1),
        input_output_aliases={3: 0},
        name="combine1",
    )(second[0], second[2], back[1], held)


def solution(mesh):
    in_specs = (
        P(None, ALL, None),
        P(None, ALL, None),
        P(("seq", "role"), None),
        P(("seq", "role"), None),
        P(),
        P(),
        P(),
        P(ALL, None, None),
        P(ALL, None, None),
    )
    return jax.shard_map(
        body, mesh=mesh, in_specs=in_specs, out_specs=P(None, ALL, None), check_vma=False
    )
```

time: 255 us -> 258 us (1.012); the launches traced: 254 us -> 255 us
  Pallas kernels: 0 us -> 111 us
  blocking collectives: 49.2 us -> 0 us
  starting transfers between devices: 4.79 us -> 36.5 us
  local copies, waits for them, and re-layouts: 33 us -> 7.97 us
  waiting for transfers between devices: 89.1 us -> 68 us
  matrix products: 49.9 us -> 29.9 us
  other arithmetic: 14.9 us -> 0.32 us
  between operations: 13.6 us -> 0.44 us
    pallas_call x0 -> x6, Pallas kernels: none -> 111 us  [the longest x1 72.7 us: assemble(): pl.pallas_call(assemble_kernel, out_shape=jax.ShapeDtypeStruct((768, bloc...]
    all_to_all x1 -> x0, blocking collectives: 49.2 us -> none  [body(): lax.all_to_all(outgoing, ('seq', 'role', 'exp'), split_axis=0, concat_axi...]
    all_gather x2 -> x0, waiting for transfers between devices: 48.2 us -> none  [the longest x1 48.2 us: body(): lax.all_gather(attn_qkv, ('seq', 'role'), axis=0, tiled=True)]
    dot_general x9 -> x2, matrix products: 49.9 us -> 29.9 us  [serve(): return jnp.dot(hidden, weight_out, preferred_element_type=F32).astype(BF16)]
    ppermute x0 -> x7, waiting for transfers between devices: none -> 17.8 us  [the longest x3 13.3 us: body(): others = [lax.ppermute(block, ALL, hop(d, 1)) for d in (1, -1, 2)]]
    all_to_all x1 -> x4, starting transfers between devices: 4.75 us -> 22.6 us  [exchange(): lax.all_to_all(values.reshape(experts, SLOTS, width), ALL, split_axis=0,...]
    ppermute x0 -> x7, starting transfers between devices: none -> 13.9 us  [the longest x3 5.95 us: body(): lax.ppermute(piece, ALL, hop(d, 0))]
    all_to_all x1 -> x4, waiting for transfers between devices: 39.5 us -> 50.2 us  [exchange(): lax.all_to_all(values.reshape(experts, SLOTS, width), ALL, split_axis=0,...]
  transfers between devices with their start and end apart: 3 -> 11, of which waited for: 2 -> 9; matrix products, arithmetic and copies ran while one was open for 21% -> 13% of each run, Pallas kernels for 0% -> 10%
where the time goes in v1:
time: 258 us; the launch traced here: 255 us
  Pallas kernels  111 us (43%)
  waiting for transfers between devices  68 us (26%)
  starting transfers between devices  36.5 us (14%)
  matrix products  29.9 us (12%)
  local copies, waits for them, and re-layouts  7.97 us (3%)
    pallas_call x1, Pallas kernels, assemble(): pl.pallas_call(assemble_kernel, out_shape=jax.ShapeDtypeStruct((768, bloc...  72.7 us
    all_to_all x4, waiting for transfers between devices, exchange(): lax.all_to_all(values.reshape(experts, SLOTS, width), ALL, split_axis=0,...  50.2 us
    dot_general x2, matrix products, serve(): return jnp.dot(hidden, weight_out, preferred_element_type=F32).astype(BF16)  29.9 us
    all_to_all x4, starting transfers between devices, exchange(): lax.all_to_all(values.reshape(experts, SLOTS, width), ALL, split_axis=0,...  22.6 us
    pallas_call x1, Pallas kernels, body(): pl.pallas_call(whole_kernel, grid=(1,), out_shape=finish_out, in_specs=[t...  14.5 us
    ppermute x3, waiting for transfers between devices, body(): others = [lax.ppermute(block, ALL, hop(d, 1)) for d in (1, -1, 2)]  13.3 us
    pallas_call x1, Pallas kernels, body(): pl.pallas_call(second_half_kernel, grid=(1,), out_shape=finish_out, in_sp...  10.9 us
    pallas_call x1, Pallas kernels, body(): pl.pallas_call(context_kernel, grid=(1,), out_shape=jax.ShapeDtypeStruct(...  6.04 us
  transfers between devices with their start and end apart: 11, of which 9 were waited for; matrix products, arithmetic and copies ran while one was open for 13% of the time, Pallas kernels for 10%

profile of v1, /device:TPU:1, one launch (start us, length us, event | category | flops | bytes accessed | tf_op | source)
XLA Modules:
  0.0 254.7 jit_solution(1884533461463411184)
XLA Ops:
  0.0 1.0 reshape.45
  2.5 2.5 collective-permute-start
  5.1 2.2 collective-permute-start.1
  7.3 1.2 collective-permute-start.2
  8.5 1.4 collective-permute-done
  10.0 3.1 %collective-permute-done.2 = bf16[48,1536]{1,0:T(8,128)(2,1)S(1)} collective-permute-done((bf16[48,1536]{1,0:T(8,128)(2,1)S(1)}, bf16[48,1536]{1,0:T(8,128)(2,1)S(1)}, u32[]{:S(2)}, u32[]{:S(2)}) %collective-permute-start.2) | collective-permute-done | bytes 147488 | tf_op jit(solution)/shard_map/ppermute | solution.py:226
  13.1 1.0 collective-permute-start.3
  14.1 1.8 collective-permute-start.4
  15.8 1.2 collective-permute-start.5
  17.1 6.3 %collective-permute-done.3.b1 = bf16[192,1536]{1,0:T(8,128)(2,1)S(1)} collective-permute-done((bf16[192,1536]{1,0:T(8,128)(2,1)S(1)}, bf16[192,1536]{1,0:T(8,128)(2,1)S(1)}, u32[]{:S(2)}, u32[]{:S(2)}) %collective-permute-start.3) | collective-permute-done | bytes 589856 | tf_op jit(solution)/shard_map/ppermute | solution.py:228
  23.4 5.6 %collective-permute-done.4.b2 = bf16[192,1536]{1,0:T(8,128)(2,1)S(1)} collective-permute-done((bf16[192,1536]{1,0:T(8,128)(2,1)S(1)}, bf16[192,1536]{1,0:T(8,128)(2,1)S(1)}, u32[]{:S(2)}, u32[]{:S(2)}) %collective-permute-start.4) | collective-permute-done | bytes 589856 | tf_op jit(solution)/shard_map/ppermute | solution.py:228
  29.0 1.4 collective-permute-done.5.b3
  31.2 72.7 %assemble.1.mine_ref.w_ref = bf16[768,1536]{1,0:T(8,128)(2,1)} custom-call(bf16[192,1536]{1,0:T(8,128)(2,1)} %copy-done.3, bf16[192,1536]{1,0:T(8,128)(2,1)} %copy-done.4, bf16[192,1536]{1,0:T(8,128)(2,1)} %copy-done.5, bf16[192,1536]{1,0:T(8,128)(2,1)} %copy-done.6), custom_call_target="tpu_custom_call" | custom-call | tf_op jit(solution)/shard_map/assemble/pallas_call | solution.py:72
  104.0 4.0 %collective-permute-start.6 = (bf16[768,1536]{1,0:T(8,128)(2,1)}, bf16[768,1536]{1,0:T(8,128)(2,1)S(1)}, u32[]{:S(2)}, u32[]{:S(2)}) collective-permute-start(bf16[768,1536]{1,0:T(8,128)(2,1)} %assemble.1.mine_ref.w_ref), channel_id=1, source_target_pairs={{0,1},{1,0},{2,3},{3,2},{4,5},{5,4},{6,7},{7,6},{8,9},{9,8},{10,11... | collective-permute-start | bytes 7077896 | tf_op jit(solution)/shard_map/ppermute | solution.py:230
  108.5 1.1 copy.13.col_ref
  110.2 6.0 %first_half.1.ctx_ref = bf16[512,384]{1,0:T(8,128)(2,1)} custom-call(bf16[2,512,768]{2,1,0:T(8,128)(2,1)} %x_ref.5, f32[1,768]{1,0:T(1,128)} %reshape.44.gain_ref, bf16[768,1536]{1,0:T(8,128)(2,1)} %assemble.1.mine_ref.w_ref), custom_call_target="tpu_custom_call" | custom-call | tf_op jit(solution)/shard_map/first_half/pallas_call | solution.py:240
  116.3 1.4 copy-done
  117.7 10.9 %second_half.1 = (bf16[512,768]{1,0:T(8,128)(2,1)}, bf16[1024,768]{1,0:T(8,128)(2,1)}, f32[512,128]{1,0:T(8,128)}) custom-call(bf16[2,512,768]{2,1,0:T(8,128)(2,1)} %x_ref.5, f32[1,768]{1,0:T(1,128)} %reshape.44.gain_ref, bf16[768,1536]{1,0:T(8,128)(2,1)} %assemble.1.mine_ref.w_ref, bf16[768,1536]{1,0:T(8,128)(2,1)} %copy-done, ...), custom_call_target="tpu_custom_call" | custom-call | tf_op jit(solution)/shard_map/second_half/pallas_call | solution.py:269
  128.6 7.8 %all-to-all-start.2 = ((bf16[128,8,768]{2,1,0:T(8,128)(2,1)}), bf16[128,8,768]{2,1,0:T(8,128)(2,1)S(1)}, u32[]{:S(2)}, u32[]{:S(2)}) async-start(bf16[128,8,768]{2,1,0:T(8,128)(2,1)} %bitcast.48), calls=%async_computation.2 | async-start | bytes 3145728 | tf_op jit(solution)/shard_map/all_to_all | solution.py:294
  136.4 14.5 %whole.1 = (bf16[512,768]{1,0:T(8,128)(2,1)}, bf16[1024,768]{1,0:T(8,128)(2,1)}, f32[512,128]{1,0:T(8,128)}) custom-call(bf16[2,512,768]{2,1,0:T(8,128)(2,1)} %x_ref.5, f32[1,768]{1,0:T(1,128)} %reshape.44.gain_ref, bf16[768,1536]{1,0:T(8,128)(2,1)} %assemble.1.mine_ref.w_ref, bf16[768,1536]{1,0:T(8,128)(2,1)} %copy-done, f32[1,768]{1,0:T(1,128)} %reshape.47.gain2_ref, ...), custom_call_target="tpu_custom_call" | custom-call | tf_op jit(solution)/shard_map/whole/pallas_call | solution.py:280
  150.9 10.0 %all-to-all-done.2 = bf16[128,8,768]{2,1,0:T(8,128)(2,1)S(1)} async-done(((bf16[128,8,768]{2,1,0:T(8,128)(2,1)}), bf16[128,8,768]{2,1,0:T(8,128)(2,1)S(1)}, u32[]{:S(2)}, u32[]{:S(2)}) %all-to-all-start.2) | async-done | bytes 1572896 | tf_op jit(solution)/shard_map/all_to_all | solution.py:294
  160.9 5.0 %all-to-all-start = ((bf16[128,8,768]{2,1,0:T(8,128)(2,1)}), bf16[128,8,768]{2,1,0:T(8,128)(2,1)S(1)}, u32[]{:S(2)}, u32[]{:S(2)}) async-start(bf16[128,8,768]{2,1,0:T(8,128)(2,1)} %bitcast.47), calls=%async_computation | async-start | bytes 3145728 | tf_op jit(solution)/shard_map/all_to_all | solution.py:294
  165.9 14.9 %fusion.14 = bf16[128,8,768]{2,1,0:T(8,128)(2,1)} fusion(bf16[1,3072,768]{2,1,0:T(8,128)(2,1)} %param.17, bf16[1,768,3072]{2,1,0:T(8,128)(2,1)} %param.16, bf16[128,8,768]{2,1,0:T(8,128)(2,1)S(1)} %all-to-all-done.2), kind=kOutput, calls=%fused_computation.12 | convolution fusion | flops 9670754304 | bytes 12582912 | tf_op jit(solution)/shard_map/dot_general | solution.py:300
  180.8 9.6 %all-to-all-done = bf16[128,8,768]{2,1,0:T(8,128)(2,1)S(1)} async-done(((bf16[128,8,768]{2,1,0:T(8,128)(2,1)}), bf16[128,8,768]{2,1,0:T(8,128)(2,1)S(1)}, u32[]{:S(2)}, u32[]{:S(2)}) %all-to-all-start) | async-done | bytes 1572896 | tf_op jit(solution)/shard_map/all_to_all | solution.py:294
  190.5 5.1 %all-to-all-start.3 = ((bf16[128,8,768]{2,1,0:T(8,128)(2,1)}), bf16[128,8,768]{2,1,0:T(8,128)(2,1)S(1)}, u32[]{:S(2)}, u32[]{:S(2)}) async-start(bf16[128,8,768]{2,1,0:T(8,128)(2,1)} %fusion.14), calls=%async_computation.3 | async-start | bytes 3145728 | tf_op jit(solution)/shard_map/all_to_all | solution.py:294
  195.5 15.0 %fusion.17 = bf16[128,8,768]{2,1,0:T(8,128)(2,1)} fusion(bf16[1,3072,768]{2,1,0:T(8,128)(2,1)} %param.17, bf16[1,768,3072]{2,1,0:T(8,128)(2,1)} %param.16, bf16[128,8,768]{2,1,0:T(8,128)(2,1)S(1)} %all-to-all-done), kind=kOutput, calls=%fused_computation.13 | convolution fusion | flops 9670754304 | bytes 12582912 | tf_op jit(solution)/shard_map/dot_general | solution.py:300
  210.5 9.6 %all-to-all-done.3 = bf16[128,8,768]{2,1,0:T(8,128)(2,1)S(1)} async-done(((bf16[128,8,768]{2,1,0:T(8,128)(2,1)}), bf16[128,8,768]{2,1,0:T(8,128)(2,1)S(1)}, u32[]{:S(2)}, u32[]{:S(2)}) %all-to-all-start.3) | async-done | bytes 1572896 | tf_op jit(solution)/shard_map/all_to_all | solution.py:294
  220.1 4.7 %all-to-all-start.1 = ((bf16[128,8,768]{2,1,0:T(8,128)(2,1)}), bf16[128,8,768]{2,1,0:T(8,128)(2,1)S(1)}, u32[]{:S(2)}, u32[]{:S(2)}) async-start(bf16[128,8,768]{2,1,0:T(8,128)(2,1)} %fusion.17), calls=%async_computation.1 | async-start | bytes 3145728 | tf_op jit(solution)/shard_map/all_to_all | solution.py:294
  224.8 3.7 %combine0.1.held_ref = bf16[2,512,768]{2,1,0:T(8,128)(2,1)} custom-call(bf16[512,768]{1,0:T(8,128)(2,1)} %get-tuple-element.14.att_ref, f32[512,128]{1,0:T(8,128)} %get-tuple-element.15.aux_ref, bf16[1024,768]{1,0:T(8,128)(2,1)} %bitcast.45), custom_call_target="tpu_custom_call" | custom-call | tf_op jit(solution)/shard_map/combine0/pallas_call | solution.py:307
  228.5 21.0 %all-to-all-done.1 = bf16[128,8,768]{2,1,0:T(8,128)(2,1)S(1)} async-done(((bf16[128,8,768]{2,1,0:T(8,128)(2,1)}), bf16[128,8,768]{2,1,0:T(8,128)(2,1)S(1)}, u32[]{:S(2)}, u32[]{:S(2)}) %all-to-all-start.1) | async-done | bytes 1572896 | tf_op jit(solution)/shard_map/all_to_all | solution.py:294
  249.6 1.2 copy-done.2
  250.7 3.7 %combine1.1 = bf16[2,512,768]{2,1,0:T(8,128)(2,1)} custom-call(bf16[512,768]{1,0:T(8,128)(2,1)} %get-tuple-element.11.att_ref, f32[512,128]{1,0:T(8,128)} %get-tuple-element.12.aux_ref, bf16[1024,768]{1,0:T(8,128)(2,1)} %bitcast.46, bf16[2,512,768]{2,1,0:T(8,128)(2,1)} %combine0.1.held_ref), custom_call_target="tpu_custom_call", output_to_operand_aliasing={{}: (3, {})} | custom-call | tf_op jit(solution)/shard_map/combine1/pallas_call | solution.py:315
  (31 shorter events, 3.6 us)
Async XLA Ops:
  0.0 107.9 %copy-start.8 = (f32[768]{0:T(1024)S(1)}, f32[768]{0:T(1024)}, u32[]{:S(2)}) copy-start(f32[768]{0:T(1024)} %param.13) | copy-start | bytes 9220
  0.0 108.5 %copy-start.7 = (s32[2,512,1]{1,2,0:T(1,128)S(1)}, s32[2,512,1]{1,2,0:T(1,128)}, u32[]{:S(2)}) copy-start(s32[2,512,1]{1,2,0:T(1,128)} %param.10) | copy-start | bytes 12292
  0.0 109.6 %copy-start.9 = (f32[768]{0:T(1024)S(1)}, f32[768]{0:T(1024)}, u32[]{:S(2)}) copy-start(f32[768]{0:T(1024)} %param.14) | copy-start | bytes 9220
  2.5 7.4 %collective-permute-start = (bf16[48,1536]{1,0:T(8,128)(2,1)S(1)}, bf16[48,1536]{1,0:T(8,128)(2,1)S(1)}, u32[]{:S(2)}, u32[]{:S(2)}) collective-permute-start(bf16[48,1536]{1,0:T(8,128)(2,1)S(1)} %bitcast.49), channel_id=1, source_target_pairs={{0,32},{1,9},{2,34},{3,11},{4,36},{5,13},{6,38},{7,15},{8,40},{9,1... | collective-permute-start | bytes 442376 | tf_op jit(solution)/shard_map/ppermute | solution.py:226
  5.1 4.9 %collective-permute-start.1 = (bf16[48,1536]{1,0:T(8,128)(2,1)S(1)}, bf16[48,1536]{1,0:T(8,128)(2,1)S(1)}, u32[]{:S(2)}, u32[]{:S(2)}) collective-permute-start(bf16[48,1536]{1,0:T(8,128)(2,1)S(1)} %bitcast.50), channel_id=1, source_target_pairs={{0,96},{1,25},{2,98},{3,27},{4,100},{5,29},{6,102},{7,31},{8,104},... | collective-permute-start | bytes 442376 | tf_op jit(solution)/shard_map/ppermute | solution.py:226
  7.3 5.8 %collective-permute-start.2 = (bf16[48,1536]{1,0:T(8,128)(2,1)S(1)}, bf16[48,1536]{1,0:T(8,128)(2,1)S(1)}, u32[]{:S(2)}, u32[]{:S(2)}) collective-permute-start(bf16[48,1536]{1,0:T(8,128)(2,1)S(1)} %bitcast.51), channel_id=1, source_target_pairs={{0,64},{1,17},{2,66},{3,19},{4,68},{5,21},{6,70},{7,23},{8,72},{9,... | collective-permute-start | bytes 442376 | tf_op jit(solution)/shard_map/ppermute | solution.py:226
  13.1 17.3 %copy-start.3 = (bf16[192,1536]{1,0:T(8,128)(2,1)}, bf16[192,1536]{1,0:T(8,128)(2,1)S(1)}, u32[]{:S(2)}) copy-start(bf16[192,1536]{1,0:T(8,128)(2,1)S(1)} %constant_dynamic-update-slice_fusion.b0) | copy-start | bytes 1769476
  13.1 10.3 %collective-permute-start.3 = (bf16[192,1536]{1,0:T(8,128)(2,1)S(1)}, bf16[192,1536]{1,0:T(8,128)(2,1)S(1)}, u32[]{:S(2)}, u32[]{:S(2)}) collective-permute-start(bf16[192,1536]{1,0:T(8,128)(2,1)S(1)} %constant_dynamic-update-slice_fusion.b0), channel_id=1, source_target_pairs={{0,8},{1,33},{2,10},{3,35},{4,12},{5,37},{6,14},{7,39},{8,16},{9,4... | collective-permute-start | bytes 1769480 | tf_op jit(solution)/shard_map/ppermute | solution.py:228
  14.1 14.9 %collective-permute-start.4 = (bf16[192,1536]{1,0:T(8,128)(2,1)S(1)}, bf16[192,1536]{1,0:T(8,128)(2,1)S(1)}, u32[]{:S(2)}, u32[]{:S(2)}) collective-permute-start(bf16[192,1536]{1,0:T(8,128)(2,1)S(1)} %constant_dynamic-update-slice_fusion.b0), channel_id=1, source_target_pairs={{0,24},{1,97},{2,26},{3,99},{4,28},{5,101},{6,30},{7,103},{8,0},{9... | collective-permute-start | bytes 1769480 | tf_op jit(solution)/shard_map/ppermute | solution.py:228
  15.8 14.6 %collective-permute-start.5 = (bf16[192,1536]{1,0:T(8,128)(2,1)S(1)}, bf16[192,1536]{1,0:T(8,128)(2,1)S(1)}, u32[]{:S(2)}, u32[]{:S(2)}) collective-permute-start(bf16[192,1536]{1,0:T(8,128)(2,1)S(1)} %constant_dynamic-update-slice_fusion.b0), channel_id=1, source_target_pairs={{0,16},{1,65},{2,18},{3,67},{4,20},{5,69},{6,22},{7,71},{8,24},{9,... | collective-permute-start | bytes 1769480 | tf_op jit(solution)/shard_map/ppermute | solution.py:228
  23.4 7.0 %copy-start.4 = (bf16[192,1536]{1,0:T(8,128)(2,1)}, bf16[192,1536]{1,0:T(8,128)(2,1)S(1)}, u32[]{:S(2)}) copy-start(bf16[192,1536]{1,0:T(8,128)(2,1)S(1)} %collective-permute-done.3.b1) | copy-start | bytes 1769476
  29.0 1.4 copy-start.5
  30.4 0.8 copy-start.6
  104.0 12.3 %collective-permute-start.6 = (bf16[768,1536]{1,0:T(8,128)(2,1)}, bf16[768,1536]{1,0:T(8,128)(2,1)S(1)}, u32[]{:S(2)}, u32[]{:S(2)}) collective-permute-start(bf16[768,1536]{1,0:T(8,128)(2,1)} %assemble.1.mine_ref.w_ref), channel_id=1, source_target_pairs={{0,1},{1,0},{2,3},{3,2},{4,5},{5,4},{6,7},{7,6},{8,9},{9,8},{10,11... | collective-permute-start | bytes 7077896 | tf_op jit(solution)/shard_map/ppermute | solution.py:230
  116.3 1.4 copy-start
  128.6 32.3 %all-to-all-start.2 = ((bf16[128,8,768]{2,1,0:T(8,128)(2,1)}), bf16[128,8,768]{2,1,0:T(8,128)(2,1)S(1)}, u32[]{:S(2)}, u32[]{:S(2)}) async-start(bf16[128,8,768]{2,1,0:T(8,128)(2,1)} %bitcast.48), calls=%async_computation.2 | async-start | bytes 3145728 | tf_op jit(solution)/shard_map/all_to_all | solution.py:294
  160.9 29.6 %all-to-all-start = ((bf16[128,8,768]{2,1,0:T(8,128)(2,1)}), bf16[128,8,768]{2,1,0:T(8,128)(2,1)S(1)}, u32[]{:S(2)}, u32[]{:S(2)}) async-start(bf16[128,8,768]{2,1,0:T(8,128)(2,1)} %bitcast.47), calls=%async_computation | async-start | bytes 3145728 | tf_op jit(solution)/shard_map/all_to_all | solution.py:294
  190.5 29.7 %all-to-all-start.3 = ((bf16[128,8,768]{2,1,0:T(8,128)(2,1)}), bf16[128,8,768]{2,1,0:T(8,128)(2,1)S(1)}, u32[]{:S(2)}, u32[]{:S(2)}) async-start(bf16[128,8,768]{2,1,0:T(8,128)(2,1)} %fusion.14), calls=%async_computation.3 | async-start | bytes 3145728 | tf_op jit(solution)/shard_map/all_to_all | solution.py:294
  220.1 4.7 %copy-start.1 = (bf16[128,8,768]{2,1,0:T(8,128)(2,1)}, bf16[128,8,768]{2,1,0:T(8,128)(2,1)S(1)}, u32[]{:S(2)}) copy-start(bf16[128,8,768]{2,1,0:T(8,128)(2,1)S(1)} %all-to-all-done.3) | copy-start | bytes 4718596
  220.1 29.4 %all-to-all-start.1 = ((bf16[128,8,768]{2,1,0:T(8,128)(2,1)}), bf16[128,8,768]{2,1,0:T(8,128)(2,1)S(1)}, u32[]{:S(2)}, u32[]{:S(2)}) async-start(bf16[128,8,768]{2,1,0:T(8,128)(2,1)} %fusion.17), calls=%async_computation.1 | async-start | bytes 3145728 | tf_op jit(solution)/shard_map/all_to_all | solution.py:294
  249.5 1.2 copy-start.2
